TPU v7x, 32 devices: a whole 2x2x4 slice. The times are simulated.
32 devices in a mesh: blk: 8 (over y, x, core), batch: 4 (over z).
Axes of the slice: x: 2, y: 2, z: 4, core: 2. Of those that a mesh axis runs over, the one named last changes fastest.
Arguments:
- query_base: bfloat16 [32, 36864], P(('batch', 'blk')), may hold values from -14 to 14
- query_latent: bfloat16 [32, 1536], P(('batch', 'blk')), may hold values from -6 to 6
- tenant_ids: int32 [32], P('batch'), may hold values from 0 to 3
- adapter_qa: bfloat16 [4, 1536, 16], replicated, may hold values from -0.15625 to 0.15625
- adapter_qb: bfloat16 [4, 16, 36864], replicated, may hold values from -0.29882812 to 0.29882812
- prefix_cache: bfloat16 [32768, 576], P('blk'), may hold values from -6 to 6
- prefix_mask: int32 [32, 256], P('batch', 'blk'), may hold values 0 or 1
- suffix_cache: bfloat16 [32, 4096, 576], P(('batch', 'blk')), may hold values from -6 to 6
- suffix_blocks: int32 [8, 4], P('blk'), may hold values from 1 to 32, 40 in all within a row
- new_latent: bfloat16 [32, 576], P(('batch', 'blk')), may hold values from -6 to 6
- value_up: bfloat16 [64, 512, 128], P('blk'), may hold values from -0.25 to 0.25
- out_weight: bfloat16 [8192, 7168], P('blk'), may hold values from -0.0625 to 0.0625
- adapter_oa: bfloat16 [4, 8192, 16], P(None, 'blk'), may hold values from -0.0625 to 0.0625
- adapter_ob: bfloat16 [4, 16, 7168], replicated, may hold values from -1.5 to 1.5
Outputs:
- attention_out: bfloat16 [32, 7168], P(('batch', 'blk'))
Inputs may be any that keep to these rules, and one draw needn't show every extreme that they name: `suffix_blocks`: each row holds 40 blocks in all, and its largest entry is exactly 32.
All inputs are finite; a program needn't handle non-finite values. No bound on the sum of `prefix_mask` on one device may be relied on, other than what follows from the above.
Results may differ from a plain program's by a relative error of at most 0.025.
Values may be sent and summed in bfloat16 or wider, within the bound.
A program may use at most 128 MiB of HBM per device.

v0:
```python
import jax
import jax.numpy as jnp
from jax import lax
from jax.sharding import PartitionSpec as P

D = 7168
H = 64
LAT = 512
QK = 192
RANK = 16
BLOCK = 128
KV = 576


floor_score = -1e30


def passed_along(block, axis, distance):
    devices = range(lax.axis_size(axis))
    route = [((i - distance) % len(devices), i) for i in devices]
    return lax.ppermute(block, axis, route)


def combine_parts(first_part, second_part):
    peak = jnp.maximum(first_part[0], second_part[0])
    first_scale = jnp.exp(first_part[0] - peak)
    second_scale = jnp.exp(second_part[0] - peak)
    totals = first_part[1] * first_scale + second_part[1] * second_scale
    sums = first_part[2] * first_scale[..., None] + second_part[2] * second_scale[..., None]
    return (peak, totals, sums)


def partial_softmax(scores, live_keys, values, per_row):
    masked = jnp.where(live_keys, scores, -jnp.inf)
    peak = jnp.maximum(jnp.max(masked, axis=-1), floor_score)
    weights = jnp.exp(masked - peak[..., None])
    totals = jnp.sum(weights, axis=-1)
    weights_low = weights.astype(jnp.bfloat16)
    if per_row:
        sums = jnp.einsum("nht,ntl->nhl", weights_low, values, preferred_element_type=jnp.float32)
    else:
        sums = jnp.einsum("nht,tl->nhl", weights_low, values, preferred_element_type=jnp.float32)
    return (peak, totals, sums)


def prefix_part(queries, mask_rows, prefix_cache, score_scale):
    count_rows = queries.shape[0]
    blocks_here = mask_rows.shape[1]
    scores = (
        jnp.einsum("nhk,tk->nht", queries, prefix_cache, preferred_element_type=jnp.float32)
        * score_scale
    )
    live_keys = jnp.broadcast_to((mask_rows > 0)[:, :, None], (count_rows, blocks_here, BLOCK))
    live_keys = live_keys.reshape(count_rows, 1, blocks_here * BLOCK)
    return partial_softmax(scores, live_keys, prefix_cache[:, :LAT], False)


def empty_parts(count_rows):
    return (
        jnp.full((count_rows, H), floor_score, jnp.float32),
        jnp.zeros((count_rows, H), jnp.float32),
        jnp.zeros((count_rows, H, LAT), jnp.float32),
    )


def on_device(
    query_base,
    query_latent,
    tenant_ids,
    adapter_qa,
    adapter_qb,
    prefix_cache,
    prefix_mask,
    suffix_cache,
    suffix_blocks,
    new_latent,
    value_up,
    out_weight,
    adapter_oa,
    adapter_ob,
):
    score_scale = QK ** (-0.5)
    blk_count = lax.axis_size("blk")
    blk_index = lax.axis_index("blk")
    batch_index = lax.axis_index("batch")
    owned_rows = query_base.shape[0]
    group_rows = owned_rows * blk_count
    tenants = adapter_qa.shape[0]
    own_tenant = lax.dynamic_slice_in_dim(tenant_ids, blk_index * owned_rows, owned_rows)
    tenant_hit = (own_tenant[:, None] == jnp.arange(tenants)[None, :]).astype(jnp.float32)
    low_every = jnp.einsum(
        "rq,tqk->rtk", query_latent, adapter_qa, preferred_element_type=jnp.float32
    )
    low_query = jnp.sum(low_every * tenant_hit[:, :, None], axis=1).astype(jnp.bfloat16)
    low_spread = (tenant_hit.astype(jnp.bfloat16)[:, :, None] * low_query[:, None, :]).reshape(
        owned_rows, tenants * RANK
    )
    delta_query = jnp.dot(
        low_spread, adapter_qb.reshape(tenants * RANK, H * KV), preferred_element_type=jnp.float32
    )
    query = (query_base.astype(jnp.float32) + delta_query).astype(jnp.bfloat16)
    query_heads = query.reshape(owned_rows, H, KV)

    def travel_step(visit_step, state):
        moving, running = state
        anchor = (blk_index - visit_step) % blk_count
        mask_rows = lax.dynamic_slice_in_dim(prefix_mask, anchor * owned_rows, owned_rows)
        fresh_part = prefix_part(
            moving.reshape(owned_rows, H, KV), mask_rows, prefix_cache, score_scale
        )
        running = combine_parts(running, fresh_part)
        moving = passed_along(moving, "blk", 1)
        running = passed_along((running[0], running[1], running[2]), "blk", 1)
        return (moving, running)

    final_state = lax.fori_loop(0, blk_count, travel_step, (query, empty_parts(owned_rows)))
    prefix_result = final_state[1]
    length_row = suffix_blocks[0]
    own_lengths = lax.dynamic_slice_in_dim(length_row, batch_index * owned_rows, owned_rows)
    slot_count = suffix_cache.shape[1]
    scores = (
        jnp.einsum("nhk,ntk->nht", query_heads, suffix_cache, preferred_element_type=jnp.float32)
        * score_scale
    )
    live_keys = jnp.arange(slot_count)[None, None, :] < (own_lengths * BLOCK)[:, None, None]
    suffix_result = partial_softmax(scores, live_keys, suffix_cache[:, :, :LAT], True)
    new_scores = (
        jnp.einsum("nhk,nk->nh", query_heads, new_latent, preferred_element_type=jnp.float32)
        * score_scale
    )
    new_values = jnp.broadcast_to(
        new_latent[:, None, :LAT].astype(jnp.float32), (owned_rows, H, LAT)
    )
    new_part = (new_scores, jnp.ones_like(new_scores), new_values)
    combined = combine_parts(combine_parts(prefix_result, suffix_result), new_part)
    context = (combined[2] / combined[1][..., None]).astype(jnp.bfloat16)
    head_rows = lax.all_to_all(context, "blk", split_axis=1, concat_axis=0, tiled=True)
    head_out = jnp.einsum("rhl,hlv->rhv", head_rows, value_up, preferred_element_type=jnp.float32)
    head_out = head_out.astype(jnp.bfloat16).reshape(group_rows, -1)
    group_hit = (tenant_ids[:, None] == jnp.arange(tenants)[None, :]).astype(jnp.float32)
    adapter_up = adapter_ob.reshape(tenants * RANK, D).astype(jnp.float32)
    projected = jnp.dot(head_out, out_weight, preferred_element_type=jnp.float32)
    low_every_out = jnp.einsum(
        "rk,tkj->rtj", head_out, adapter_oa, preferred_element_type=jnp.float32
    )
    low_spread_out = (low_every_out * group_hit[:, :, None]).reshape(
        lax.axis_size("blk") * owned_rows, tenants * RANK
    )
    return lax.psum_scatter(
        (projected + jnp.dot(low_spread_out, adapter_up, precision=lax.Precision.HIGHEST)).astype(
            jnp.bfloat16
        ),
        "blk",
        scatter_dimension=0,
        tiled=True,
    )


def solution(mesh):
    placed = (
        P(("batch", "blk"), None),
        P(("batch", "blk"), None),
        P("batch"),
        P(),
        P(),
        P("blk", None),
        P("batch", "blk"),
        P(("batch", "blk"), None, None),
        P("blk", None),
        P(("batch", "blk"), None),
        P("blk", None, None),
        P("blk", None),
        P(None, "blk", None),
        P(),
    )
    return jax.shard_map(
        on_device, mesh=mesh, in_specs=placed, out_specs=P(("batch", "blk"), None), check_vma=False
    )
```

profile of v0, /device:TPU:0, one launch (start us, length us, event | category | flops | bytes accessed | tf_op | source)
XLA Modules:
  0.0 224.7 jit_solution(18082579267390969847)
XLA Ops:
  12.9 3.2 %fusion.80 = (bf16[36864]{0:T(1024)(128)(2,1)S(1)}, bf16[1,36864]{1,0:T(2,128)(2,1)S(1)}) fusion(bf16[64,1]{0,1:T(2,128)(2,1)S(1)} %reshape.366, bf16[64,36864]{1,0:T(8,128)(2,1)} %bitcast.182, bf16[1,36864]{1,0:T(2,128)(2,1)} %param.16), kind=kOutput, calls=%fused_computation.86 | convolution fusion | flops 4829184 | bytes 4939904 | tf_op jit(solution)/shard_map/dot_general | solution.py:98
  16.2 3.5 %fusion.82 = (f32[64]{0:T(128)S(1)}, f32[64,4096]{1,0:T(8,128)S(1)}) fusion(bf16[64,576]{1,0:T(8,128)(2,1)S(1)} %reshape.358, bf16[1,4096,576]{1,2,0:T(8,128)(2,1)} %param.23, pred[4096]{0:T(1024)(128)(4,1)S(1)} %iota_compare_fusion), kind=kOutput, calls=%fused_computation.88 | convolution fusion | flops 302776256 | bytes 5845248 | tf_op jit(solution)/shard_map/nhk,ntk->nht/dot_general | solution.py:122
  20.7 119.1 %while.21 = (s32[]{:T(128)}, bf16[1,36864]{1,0:T(2,128)(2,1)S(1)}, f32[1,64]{1,0:T(1,128)S(1)}, f32[1,64]{1,0:T(1,128)S(1)}, f32[1,64,512]{2,1,0:T(8,128)}, /*in...) while((s32[]{:T(128)}, bf16[1,36864]{1,0:T(2,128)(2,1)S(1)}, ...), condition=%wide.region_4.5_spmd, body=%wide.region_1.4_spmd.sunk | while | flops 572359104 | bytes 32546200 | solution.py:116
  22.2 3.6 %fusion.109 = (f32[64]{0:T(128)S(1)}, f32[64,4096]{1,0:T(8,128)S(1)}) fusion(bf16[64,576]{1,0:T(8,128)(2,1)S(1)} %reshape.381, bf16[4096,576]{0,1:T(8,128)(2,1)} %get-tuple-element.336, pred[4096]{0:T(1024)(128)(4,1)S(1)} %broadcast_bitcast_fusion.2), kind=kOutput, calls=%fused_computation.85.clone.1 | convolution fusion | flops 302776256 | bytes 5845248 | tf_op jit(solution)/shard_map/while/body/eval_jaxpr/nhk,tk->nht/dot_general | solution.py:50
  29.0 2.6 %collective-permute-start = (bf16[1,36864]{1,0:T(2,128)(2,1)S(1)}, bf16[1,36864]{1,0:T(2,128)(2,1)S(1)}, u32[]{:S(2)}, u32[]{:S(2)}) collective-permute-start(bf16[1,36864]{1,0:T(2,128)(2,1)S(1)} %copy.35), channel_id=1, source_target_pairs={{28,0},{0,4},{4,8},{8,12},{12,16},{16,20},{20,24},{24,28},{29,1},{... | collective-permute-start | bytes 221192 | tf_op jit(solution)/shard_map/while/body/eval_jaxpr/ppermute | solution.py:21
  33.2 3.0 %collective-permute-done.1 = f32[1,64]{1,0:T(1,128)S(1)} collective-permute-done((f32[1,64]{1,0:T(1,128)S(1)}, f32[1,64]{1,0:T(1,128)S(1)}, u32[]{:S(2)}, u32[]{:S(2)}) %collective-permute-start.1) | collective-permute-done | bytes 288 | tf_op jit(solution)/shard_map/while/body/eval_jaxpr/ppermute | solution.py:21
  37.7 3.6 %fusion.109 = (f32[64]{0:T(128)S(1)}, f32[64,4096]{1,0:T(8,128)S(1)}) fusion(bf16[64,576]{1,0:T(8,128)(2,1)S(1)} %reshape.381, bf16[4096,576]{0,1:T(8,128)(2,1)} %get-tuple-element.336, pred[4096]{0:T(1024)(128)(4,1)S(1)} %broadcast_bitcast_fusion.2), kind=kOutput, calls=%fused_computation.85.clone.1 | convolution fusion | flops 302776256 | bytes 5845248 | tf_op jit(solution)/shard_map/while/body/eval_jaxpr/nhk,tk->nht/dot_general | solution.py:50
  45.6 2.4 %collective-permute-start.2 = (f32[1,64]{1,0:T(1,128)S(1)}, f32[1,64]{1,0:T(1,128)S(1)}, u32[]{:S(2)}, u32[]{:S(2)}) collective-permute-start(f32[1,64]{1,0:T(1,128)S(1)} %get-tuple-element.300), channel_id=1, source_target_pairs={{28,0},{0,4},{4,8},{8,12},{12,16},{16,20},{20,24},{24,28},{29,1},{... | collective-permute-start | bytes 776 | tf_op jit(solution)/shard_map/while/body/eval_jaxpr/ppermute | solution.py:21
  48.0 3.0 %collective-permute-done.1 = f32[1,64]{1,0:T(1,128)S(1)} collective-permute-done((f32[1,64]{1,0:T(1,128)S(1)}, f32[1,64]{1,0:T(1,128)S(1)}, u32[]{:S(2)}, u32[]{:S(2)}) %collective-permute-start.1) | collective-permute-done | bytes 288 | tf_op jit(solution)/shard_map/while/body/eval_jaxpr/ppermute | solution.py:21
  52.5 3.6 %fusion.109 = (f32[64]{0:T(128)S(1)}, f32[64,4096]{1,0:T(8,128)S(1)}) fusion(bf16[64,576]{1,0:T(8,128)(2,1)S(1)} %reshape.381, bf16[4096,576]{0,1:T(8,128)(2,1)} %get-tuple-element.336, pred[4096]{0:T(1024)(128)(4,1)S(1)} %broadcast_bitcast_fusion.2), kind=kOutput, calls=%fused_computation.85.clone.1 | convolution fusion | flops 302776256 | bytes 5845248 | tf_op jit(solution)/shard_map/while/body/eval_jaxpr/nhk,tk->nht/dot_general | solution.py:50
  59.5 3.3 %collective-permute-start.2 = (f32[1,64]{1,0:T(1,128)S(1)}, f32[1,64]{1,0:T(1,128)S(1)}, u32[]{:S(2)}, u32[]{:S(2)}) collective-permute-start(f32[1,64]{1,0:T(1,128)S(1)} %get-tuple-element.300), channel_id=1, source_target_pairs={{28,0},{0,4},{4,8},{8,12},{12,16},{16,20},{20,24},{24,28},{29,1},{... | collective-permute-start | bytes 776 | tf_op jit(solution)/shard_map/while/body/eval_jaxpr/ppermute | solution.py:21
  62.8 3.0 %collective-permute-done.1 = f32[1,64]{1,0:T(1,128)S(1)} collective-permute-done((f32[1,64]{1,0:T(1,128)S(1)}, f32[1,64]{1,0:T(1,128)S(1)}, u32[]{:S(2)}, u32[]{:S(2)}) %collective-permute-start.1) | collective-permute-done | bytes 288 | tf_op jit(solution)/shard_map/while/body/eval_jaxpr/ppermute | solution.py:21
  67.3 3.6 %fusion.109 = (f32[64]{0:T(128)S(1)}, f32[64,4096]{1,0:T(8,128)S(1)}) fusion(bf16[64,576]{1,0:T(8,128)(2,1)S(1)} %reshape.381, bf16[4096,576]{0,1:T(8,128)(2,1)} %get-tuple-element.336, pred[4096]{0:T(1024)(128)(4,1)S(1)} %broadcast_bitcast_fusion.2), kind=kOutput, calls=%fused_computation.85.clone.1 | convolution fusion | flops 302776256 | bytes 5845248 | tf_op jit(solution)/shard_map/while/body/eval_jaxpr/nhk,tk->nht/dot_general | solution.py:50
  74.2 3.4 %collective-permute-start.2 = (f32[1,64]{1,0:T(1,128)S(1)}, f32[1,64]{1,0:T(1,128)S(1)}, u32[]{:S(2)}, u32[]{:S(2)}) collective-permute-start(f32[1,64]{1,0:T(1,128)S(1)} %get-tuple-element.300), channel_id=1, source_target_pairs={{28,0},{0,4},{4,8},{8,12},{12,16},{16,20},{20,24},{24,28},{29,1},{... | collective-permute-start | bytes 776 | tf_op jit(solution)/shard_map/while/body/eval_jaxpr/ppermute | solution.py:21
  77.6 3.0 %collective-permute-done.1 = f32[1,64]{1,0:T(1,128)S(1)} collective-permute-done((f32[1,64]{1,0:T(1,128)S(1)}, f32[1,64]{1,0:T(1,128)S(1)}, u32[]{:S(2)}, u32[]{:S(2)}) %collective-permute-start.1) | collective-permute-done | bytes 288 | tf_op jit(solution)/shard_map/while/body/eval_jaxpr/ppermute | solution.py:21
  82.1 3.6 %fusion.109 = (f32[64]{0:T(128)S(1)}, f32[64,4096]{1,0:T(8,128)S(1)}) fusion(bf16[64,576]{1,0:T(8,128)(2,1)S(1)} %reshape.381, bf16[4096,576]{0,1:T(8,128)(2,1)} %get-tuple-element.336, pred[4096]{0:T(1024)(128)(4,1)S(1)} %broadcast_bitcast_fusion.2), kind=kOutput, calls=%fused_computation.85.clone.1 | convolution fusion | flops 302776256 | bytes 5845248 | tf_op jit(solution)/shard_map/while/body/eval_jaxpr/nhk,tk->nht/dot_general | solution.py:50
  89.0 3.4 %collective-permute-start.2 = (f32[1,64]{1,0:T(1,128)S(1)}, f32[1,64]{1,0:T(1,128)S(1)}, u32[]{:S(2)}, u32[]{:S(2)}) collective-permute-start(f32[1,64]{1,0:T(1,128)S(1)} %get-tuple-element.300), channel_id=1, source_target_pairs={{28,0},{0,4},{4,8},{8,12},{12,16},{16,20},{20,24},{24,28},{29,1},{... | collective-permute-start | bytes 776 | tf_op jit(solution)/shard_map/while/body/eval_jaxpr/ppermute | solution.py:21
  92.4 3.0 %collective-permute-done.1 = f32[1,64]{1,0:T(1,128)S(1)} collective-permute-done((f32[1,64]{1,0:T(1,128)S(1)}, f32[1,64]{1,0:T(1,128)S(1)}, u32[]{:S(2)}, u32[]{:S(2)}) %collective-permute-start.1) | collective-permute-done | bytes 288 | tf_op jit(solution)/shard_map/while/body/eval_jaxpr/ppermute | solution.py:21
  96.9 3.6 %fusion.109 = (f32[64]{0:T(128)S(1)}, f32[64,4096]{1,0:T(8,128)S(1)}) fusion(bf16[64,576]{1,0:T(8,128)(2,1)S(1)} %reshape.381, bf16[4096,576]{0,1:T(8,128)(2,1)} %get-tuple-element.336, pred[4096]{0:T(1024)(128)(4,1)S(1)} %broadcast_bitcast_fusion.2), kind=kOutput, calls=%fused_computation.85.clone.1 | convolution fusion | flops 302776256 | bytes 5845248 | tf_op jit(solution)/shard_map/while/body/eval_jaxpr/nhk,tk->nht/dot_general | solution.py:50
  103.8 3.4 %collective-permute-start.2 = (f32[1,64]{1,0:T(1,128)S(1)}, f32[1,64]{1,0:T(1,128)S(1)}, u32[]{:S(2)}, u32[]{:S(2)}) collective-permute-start(f32[1,64]{1,0:T(1,128)S(1)} %get-tuple-element.300), channel_id=1, source_target_pairs={{28,0},{0,4},{4,8},{8,12},{12,16},{16,20},{20,24},{24,28},{29,1},{... | collective-permute-start | bytes 776 | tf_op jit(solution)/shard_map/while/body/eval_jaxpr/ppermute | solution.py:21
  107.2 3.0 %collective-permute-done.1 = f32[1,64]{1,0:T(1,128)S(1)} collective-permute-done((f32[1,64]{1,0:T(1,128)S(1)}, f32[1,64]{1,0:T(1,128)S(1)}, u32[]{:S(2)}, u32[]{:S(2)}) %collective-permute-start.1) | collective-permute-done | bytes 288 | tf_op jit(solution)/shard_map/while/body/eval_jaxpr/ppermute | solution.py:21
  111.7 3.6 %fusion.109 = (f32[64]{0:T(128)S(1)}, f32[64,4096]{1,0:T(8,128)S(1)}) fusion(bf16[64,576]{1,0:T(8,128)(2,1)S(1)} %reshape.381, bf16[4096,576]{0,1:T(8,128)(2,1)} %get-tuple-element.336, pred[4096]{0:T(1024)(128)(4,1)S(1)} %broadcast_bitcast_fusion.2), kind=kOutput, calls=%fused_computation.85.clone.1 | convolution fusion | flops 302776256 | bytes 5845248 | tf_op jit(solution)/shard_map/while/body/eval_jaxpr/nhk,tk->nht/dot_general | solution.py:50
  118.6 3.4 %collective-permute-start.2 = (f32[1,64]{1,0:T(1,128)S(1)}, f32[1,64]{1,0:T(1,128)S(1)}, u32[]{:S(2)}, u32[]{:S(2)}) collective-permute-start(f32[1,64]{1,0:T(1,128)S(1)} %get-tuple-element.300), channel_id=1, source_target_pairs={{28,0},{0,4},{4,8},{8,12},{12,16},{16,20},{20,24},{24,28},{29,1},{... | collective-permute-start | bytes 776 | tf_op jit(solution)/shard_map/while/body/eval_jaxpr/ppermute | solution.py:21
  122.0 3.0 %collective-permute-done.1 = f32[1,64]{1,0:T(1,128)S(1)} collective-permute-done((f32[1,64]{1,0:T(1,128)S(1)}, f32[1,64]{1,0:T(1,128)S(1)}, u32[]{:S(2)}, u32[]{:S(2)}) %collective-permute-start.1) | collective-permute-done | bytes 288 | tf_op jit(solution)/shard_map/while/body/eval_jaxpr/ppermute | solution.py:21
  126.5 3.6 %fusion.109 = (f32[64]{0:T(128)S(1)}, f32[64,4096]{1,0:T(8,128)S(1)}) fusion(bf16[64,576]{1,0:T(8,128)(2,1)S(1)} %reshape.381, bf16[4096,576]{0,1:T(8,128)(2,1)} %get-tuple-element.336, pred[4096]{0:T(1024)(128)(4,1)S(1)} %broadcast_bitcast_fusion.2), kind=kOutput, calls=%fused_computation.85.clone.1 | convolution fusion | flops 302776256 | bytes 5845248 | tf_op jit(solution)/shard_map/while/body/eval_jaxpr/nhk,tk->nht/dot_general | solution.py:50
  133.4 3.4 %collective-permute-start.2 = (f32[1,64]{1,0:T(1,128)S(1)}, f32[1,64]{1,0:T(1,128)S(1)}, u32[]{:S(2)}, u32[]{:S(2)}) collective-permute-start(f32[1,64]{1,0:T(1,128)S(1)} %get-tuple-element.300), channel_id=1, source_target_pairs={{28,0},{0,4},{4,8},{8,12},{12,16},{16,20},{20,24},{24,28},{29,1},{... | collective-permute-start | bytes 776 | tf_op jit(solution)/shard_map/while/body/eval_jaxpr/ppermute | solution.py:21
  136.8 3.0 %collective-permute-done.1 = f32[1,64]{1,0:T(1,128)S(1)} collective-permute-done((f32[1,64]{1,0:T(1,128)S(1)}, f32[1,64]{1,0:T(1,128)S(1)}, u32[]{:S(2)}, u32[]{:S(2)}) %collective-permute-start.1) | collective-permute-done | bytes 288 | tf_op jit(solution)/shard_map/while/body/eval_jaxpr/ppermute | solution.py:21
  140.0 3.8 %fusion.53 = bf16[1,64,512]{2,1,0:T(8,128)(2,1)S(1)} fusion(bf16[1,4096,576]{1,2,0:T(8,128)(2,1)} %param.23, f32[64,4096]{1,0:T(8,128)S(1)} %get-tuple-element.239, f32[64]{0:T(128)S(1)} %broadcast_maximum_fusion.1, f32[1,64,512]{2,1,0:T(8,128)} %get-tuple-element.206, f32[64]{0:T(128)S(1)} %get-tuple-element.232, f32[64]{0:T(128)S(1)} %get-tuple-element.233, ...), kind=kOutput, calls=%fused_computation.45 | convolution fusion | flops 269221888 | bytes 5443072 | tf_op jit(solution)/shard_map/nht,ntl->nhl/dot_general | solution.py:40
  146.1 3.5 %all-to-all-start = ((bf16[8,2,2048]{2,1,0:T(2,128)(2,1)}), bf16[8,2,2048]{2,1,0:T(2,128)(2,1)S(1)}, u32[]{:S(2)}, u32[]{:S(2)}) async-start(bf16[8,2,2048]{2,1,0:T(2,128)(2,1)} %reshape.378), calls=%async_computation | async-start | bytes 131072 | tf_op jit(solution)/shard_map/all_to_all | solution.py:137
  149.7 5.0 %all-to-all-done = bf16[8,2,2048]{2,1,0:T(2,128)(2,1)S(1)} async-done(((bf16[8,2,2048]{2,1,0:T(2,128)(2,1)}), bf16[8,2,2048]{2,1,0:T(2,128)(2,1)S(1)}, u32[]{:S(2)}, u32[]{:S(2)}) %all-to-all-start) | async-done | bytes 65568 | tf_op jit(solution)/shard_map/all_to_all | solution.py:137
  156.3 7.8 %fusion.21 = bf16[8,7168]{1,0:T(8,128)(2,1)} fusion(f32[8,7168]{1,0:T(8,128)S(1)} %convolution_bitcast_fusion, bf16[1024,7168]{1,0:T(8,128)(2,1)} %param.27, bf16[8,8,128]{2,1,0:T(8,128)(2,1)S(1)} %convolution_convert_fusion), kind=kOutput, calls=%fused_computation.26 | convolution fusion | flops 117555200 | bytes 15040512 | tf_op jit(solution)/shard_map/dot_general | solution.py:142
  164.8 50.9 %all-reduce.3.cloned.1.call-done = bf16[8,7168]{1,0:T(8,128)(2,1)} async-done(((bf16[8,7168]{1,0:T(8,128)(2,1)}), bf16[8,7168]{1,0:T(8,128)(2,1)}) %all-reduce.3.cloned.1.call-update) | async-done | bytes 114704
  (178 shorter events, 54.7 us)
Async XLA Ops:
  28.5 7.7 %collective-permute-start.3 = (f32[1,64,512]{2,1,0:T(8,128)S(1)}, f32[1,64,512]{2,1,0:T(8,128)}, u32[]{:S(2)}, u32[]{:S(2)}) collective-permute-start(f32[1,64,512]{2,1,0:T(8,128)S(1)} %fusion.112), channel_id=1, source_target_pairs={{28,0},{0,4},{4,8},{8,12},{12,16},{16,20},{20,24},{24,28},{29,1},{... | collective-permute-start | bytes 393224 | tf_op jit(solution)/shard_map/while/body/eval_jaxpr/ppermute | solution.py:21
  29.0 7.2 %collective-permute-start = (bf16[1,36864]{1,0:T(2,128)(2,1)S(1)}, bf16[1,36864]{1,0:T(2,128)(2,1)S(1)}, u32[]{:S(2)}, u32[]{:S(2)}) collective-permute-start(bf16[1,36864]{1,0:T(2,128)(2,1)S(1)} %copy.35), channel_id=1, source_target_pairs={{28,0},{0,4},{4,8},{8,12},{12,16},{16,20},{20,24},{24,28},{29,1},{... | collective-permute-start | bytes 221192 | tf_op jit(solution)/shard_map/while/body/eval_jaxpr/ppermute | solution.py:21
  44.0 7.0 %collective-permute-start.3 = (f32[1,64,512]{2,1,0:T(8,128)S(1)}, f32[1,64,512]{2,1,0:T(8,128)}, u32[]{:S(2)}, u32[]{:S(2)}) collective-permute-start(f32[1,64,512]{2,1,0:T(8,128)S(1)} %fusion.112), channel_id=1, source_target_pairs={{28,0},{0,4},{4,8},{8,12},{12,16},{16,20},{20,24},{24,28},{29,1},{... | collective-permute-start | bytes 393224 | tf_op jit(solution)/shard_map/while/body/eval_jaxpr/ppermute | solution.py:21
  44.1 6.9 %collective-permute-start = (bf16[1,36864]{1,0:T(2,128)(2,1)S(1)}, bf16[1,36864]{1,0:T(2,128)(2,1)S(1)}, u32[]{:S(2)}, u32[]{:S(2)}) collective-permute-start(bf16[1,36864]{1,0:T(2,128)(2,1)S(1)} %copy.35), channel_id=1, source_target_pairs={{28,0},{0,4},{4,8},{8,12},{12,16},{16,20},{20,24},{24,28},{29,1},{... | collective-permute-start | bytes 221192 | tf_op jit(solution)/shard_map/while/body/eval_jaxpr/ppermute | solution.py:21
  45.5 5.5 %collective-permute-start.1 = (f32[1,64]{1,0:T(1,128)S(1)}, f32[1,64]{1,0:T(1,128)S(1)}, u32[]{:S(2)}, u32[]{:S(2)}) collective-permute-start(f32[1,64]{1,0:T(1,128)S(1)} %get-tuple-element.299), channel_id=1, source_target_pairs={{28,0},{0,4},{4,8},{8,12},{12,16},{16,20},{20,24},{24,28},{29,1},{... | collective-permute-start | bytes 776 | tf_op jit(solution)/shard_map/while/body/eval_jaxpr/ppermute | solution.py:21
  45.6 5.4 %collective-permute-start.2 = (f32[1,64]{1,0:T(1,128)S(1)}, f32[1,64]{1,0:T(1,128)S(1)}, u32[]{:S(2)}, u32[]{:S(2)}) collective-permute-start(f32[1,64]{1,0:T(1,128)S(1)} %get-tuple-element.300), channel_id=1, source_target_pairs={{28,0},{0,4},{4,8},{8,12},{12,16},{16,20},{20,24},{24,28},{29,1},{... | collective-permute-start | bytes 776 | tf_op jit(solution)/shard_map/while/body/eval_jaxpr/ppermute | solution.py:21
  58.8 7.0 %collective-permute-start.3 = (f32[1,64,512]{2,1,0:T(8,128)S(1)}, f32[1,64,512]{2,1,0:T(8,128)}, u32[]{:S(2)}, u32[]{:S(2)}) collective-permute-start(f32[1,64,512]{2,1,0:T(8,128)S(1)} %fusion.112), channel_id=1, source_target_pairs={{28,0},{0,4},{4,8},{8,12},{12,16},{16,20},{20,24},{24,28},{29,1},{... | collective-permute-start | bytes 393224 | tf_op jit(solution)/shard_map/while/body/eval_jaxpr/ppermute | solution.py:21
  58.9 6.9 %collective-permute-start = (bf16[1,36864]{1,0:T(2,128)(2,1)S(1)}, bf16[1,36864]{1,0:T(2,128)(2,1)S(1)}, u32[]{:S(2)}, u32[]{:S(2)}) collective-permute-start(bf16[1,36864]{1,0:T(2,128)(2,1)S(1)} %copy.35), channel_id=1, source_target_pairs={{28,0},{0,4},{4,8},{8,12},{12,16},{16,20},{20,24},{24,28},{29,1},{... | collective-permute-start | bytes 221192 | tf_op jit(solution)/shard_map/while/body/eval_jaxpr/ppermute | solution.py:21
  59.4 6.4 %collective-permute-start.1 = (f32[1,64]{1,0:T(1,128)S(1)}, f32[1,64]{1,0:T(1,128)S(1)}, u32[]{:S(2)}, u32[]{:S(2)}) collective-permute-start(f32[1,64]{1,0:T(1,128)S(1)} %get-tuple-element.299), channel_id=1, source_target_pairs={{28,0},{0,4},{4,8},{8,12},{12,16},{16,20},{20,24},{24,28},{29,1},{... | collective-permute-start | bytes 776 | tf_op jit(solution)/shard_map/while/body/eval_jaxpr/ppermute | solution.py:21
  59.5 6.3 %collective-permute-start.2 = (f32[1,64]{1,0:T(1,128)S(1)}, f32[1,64]{1,0:T(1,128)S(1)}, u32[]{:S(2)}, u32[]{:S(2)}) collective-permute-start(f32[1,64]{1,0:T(1,128)S(1)} %get-tuple-element.300), channel_id=1, source_target_pairs={{28,0},{0,4},{4,8},{8,12},{12,16},{16,20},{20,24},{24,28},{29,1},{... | collective-permute-start | bytes 776 | tf_op jit(solution)/shard_map/while/body/eval_jaxpr/ppermute | solution.py:21
  73.6 7.0 %collective-permute-start.3 = (f32[1,64,512]{2,1,0:T(8,128)S(1)}, f32[1,64,512]{2,1,0:T(8,128)}, u32[]{:S(2)}, u32[]{:S(2)}) collective-permute-start(f32[1,64,512]{2,1,0:T(8,128)S(1)} %fusion.112), channel_id=1, source_target_pairs={{28,0},{0,4},{4,8},{8,12},{12,16},{16,20},{20,24},{24,28},{29,1},{... | collective-permute-start | bytes 393224 | tf_op jit(solution)/shard_map/while/body/eval_jaxpr/ppermute | solution.py:21
  73.7 6.9 %collective-permute-start = (bf16[1,36864]{1,0:T(2,128)(2,1)S(1)}, bf16[1,36864]{1,0:T(2,128)(2,1)S(1)}, u32[]{:S(2)}, u32[]{:S(2)}) collective-permute-start(bf16[1,36864]{1,0:T(2,128)(2,1)S(1)} %copy.35), channel_id=1, source_target_pairs={{28,0},{0,4},{4,8},{8,12},{12,16},{16,20},{20,24},{24,28},{29,1},{... | collective-permute-start | bytes 221192 | tf_op jit(solution)/shard_map/while/body/eval_jaxpr/ppermute | solution.py:21
  73.7 6.8 %collective-permute-start.1 = (f32[1,64]{1,0:T(1,128)S(1)}, f32[1,64]{1,0:T(1,128)S(1)}, u32[]{:S(2)}, u32[]{:S(2)}) collective-permute-start(f32[1,64]{1,0:T(1,128)S(1)} %get-tuple-element.299), channel_id=1, source_target_pairs={{28,0},{0,4},{4,8},{8,12},{12,16},{16,20},{20,24},{24,28},{29,1},{... | collective-permute-start | bytes 776 | tf_op jit(solution)/shard_map/while/body/eval_jaxpr/ppermute | solution.py:21
  74.2 6.4 %collective-permute-start.2 = (f32[1,64]{1,0:T(1,128)S(1)}, f32[1,64]{1,0:T(1,128)S(1)}, u32[]{:S(2)}, u32[]{:S(2)}) collective-permute-start(f32[1,64]{1,0:T(1,128)S(1)} %get-tuple-element.300), channel_id=1, source_target_pairs={{28,0},{0,4},{4,8},{8,12},{12,16},{16,20},{20,24},{24,28},{29,1},{... | collective-permute-start | bytes 776 | tf_op jit(solution)/shard_map/while/body/eval_jaxpr/ppermute | solution.py:21
  88.4 7.0 %collective-permute-start.3 = (f32[1,64,512]{2,1,0:T(8,128)S(1)}, f32[1,64,512]{2,1,0:T(8,128)}, u32[]{:S(2)}, u32[]{:S(2)}) collective-permute-start(f32[1,64,512]{2,1,0:T(8,128)S(1)} %fusion.112), channel_id=1, source_target_pairs={{28,0},{0,4},{4,8},{8,12},{12,16},{16,20},{20,24},{24,28},{29,1},{... | collective-permute-start | bytes 393224 | tf_op jit(solution)/shard_map/while/body/eval_jaxpr/ppermute | solution.py:21
  88.5 6.9 %collective-permute-start = (bf16[1,36864]{1,0:T(2,128)(2,1)S(1)}, bf16[1,36864]{1,0:T(2,128)(2,1)S(1)}, u32[]{:S(2)}, u32[]{:S(2)}) collective-permute-start(bf16[1,36864]{1,0:T(2,128)(2,1)S(1)} %copy.35), channel_id=1, source_target_pairs={{28,0},{0,4},{4,8},{8,12},{12,16},{16,20},{20,24},{24,28},{29,1},{... | collective-permute-start | bytes 221192 | tf_op jit(solution)/shard_map/while/body/eval_jaxpr/ppermute | solution.py:21
  88.6 6.8 %collective-permute-start.1 = (f32[1,64]{1,0:T(1,128)S(1)}, f32[1,64]{1,0:T(1,128)S(1)}, u32[]{:S(2)}, u32[]{:S(2)}) collective-permute-start(f32[1,64]{1,0:T(1,128)S(1)} %get-tuple-element.299), channel_id=1, source_target_pairs={{28,0},{0,4},{4,8},{8,12},{12,16},{16,20},{20,24},{24,28},{29,1},{... | collective-permute-start | bytes 776 | tf_op jit(solution)/shard_map/while/body/eval_jaxpr/ppermute | solution.py:21
  89.0 6.4 %collective-permute-start.2 = (f32[1,64]{1,0:T(1,128)S(1)}, f32[1,64]{1,0:T(1,128)S(1)}, u32[]{:S(2)}, u32[]{:S(2)}) collective-permute-start(f32[1,64]{1,0:T(1,128)S(1)} %get-tuple-element.300), channel_id=1, source_target_pairs={{28,0},{0,4},{4,8},{8,12},{12,16},{16,20},{20,24},{24,28},{29,1},{... | collective-permute-start | bytes 776 | tf_op jit(solution)/shard_map/while/body/eval_jaxpr/ppermute | solution.py:21
  103.2 7.0 %collective-permute-start.3 = (f32[1,64,512]{2,1,0:T(8,128)S(1)}, f32[1,64,512]{2,1,0:T(8,128)}, u32[]{:S(2)}, u32[]{:S(2)}) collective-permute-start(f32[1,64,512]{2,1,0:T(8,128)S(1)} %fusion.112), channel_id=1, source_target_pairs={{28,0},{0,4},{4,8},{8,12},{12,16},{16,20},{20,24},{24,28},{29,1},{... | collective-permute-start | bytes 393224 | tf_op jit(solution)/shard_map/while/body/eval_jaxpr/ppermute | solution.py:21
  103.3 6.9 %collective-permute-start = (bf16[1,36864]{1,0:T(2,128)(2,1)S(1)}, bf16[1,36864]{1,0:T(2,128)(2,1)S(1)}, u32[]{:S(2)}, u32[]{:S(2)}) collective-permute-start(bf16[1,36864]{1,0:T(2,128)(2,1)S(1)} %copy.35), channel_id=1, source_target_pairs={{28,0},{0,4},{4,8},{8,12},{12,16},{16,20},{20,24},{24,28},{29,1},{... | collective-permute-start | bytes 221192 | tf_op jit(solution)/shard_map/while/body/eval_jaxpr/ppermute | solution.py:21
  103.4 6.8 %collective-permute-start.1 = (f32[1,64]{1,0:T(1,128)S(1)}, f32[1,64]{1,0:T(1,128)S(1)}, u32[]{:S(2)}, u32[]{:S(2)}) collective-permute-start(f32[1,64]{1,0:T(1,128)S(1)} %get-tuple-element.299), channel_id=1, source_target_pairs={{28,0},{0,4},{4,8},{8,12},{12,16},{16,20},{20,24},{24,28},{29,1},{... | collective-permute-start | bytes 776 | tf_op jit(solution)/shard_map/while/body/eval_jaxpr/ppermute | solution.py:21
  103.8 6.4 %collective-permute-start.2 = (f32[1,64]{1,0:T(1,128)S(1)}, f32[1,64]{1,0:T(1,128)S(1)}, u32[]{:S(2)}, u32[]{:S(2)}) collective-permute-start(f32[1,64]{1,0:T(1,128)S(1)} %get-tuple-element.300), channel_id=1, source_target_pairs={{28,0},{0,4},{4,8},{8,12},{12,16},{16,20},{20,24},{24,28},{29,1},{... | collective-permute-start | bytes 776 | tf_op jit(solution)/shard_map/while/body/eval_jaxpr/ppermute | solution.py:21
  118.0 7.0 %collective-permute-start.3 = (f32[1,64,512]{2,1,0:T(8,128)S(1)}, f32[1,64,512]{2,1,0:T(8,128)}, u32[]{:S(2)}, u32[]{:S(2)}) collective-permute-start(f32[1,64,512]{2,1,0:T(8,128)S(1)} %fusion.112), channel_id=1, source_target_pairs={{28,0},{0,4},{4,8},{8,12},{12,16},{16,20},{20,24},{24,28},{29,1},{... | collective-permute-start | bytes 393224 | tf_op jit(solution)/shard_map/while/body/eval_jaxpr/ppermute | solution.py:21
  118.1 6.9 %collective-permute-start = (bf16[1,36864]{1,0:T(2,128)(2,1)S(1)}, bf16[1,36864]{1,0:T(2,128)(2,1)S(1)}, u32[]{:S(2)}, u32[]{:S(2)}) collective-permute-start(bf16[1,36864]{1,0:T(2,128)(2,1)S(1)} %copy.35), channel_id=1, source_target_pairs={{28,0},{0,4},{4,8},{8,12},{12,16},{16,20},{20,24},{24,28},{29,1},{... | collective-permute-start | bytes 221192 | tf_op jit(solution)/shard_map/while/body/eval_jaxpr/ppermute | solution.py:21
  118.2 6.8 %collective-permute-start.1 = (f32[1,64]{1,0:T(1,128)S(1)}, f32[1,64]{1,0:T(1,128)S(1)}, u32[]{:S(2)}, u32[]{:S(2)}) collective-permute-start(f32[1,64]{1,0:T(1,128)S(1)} %get-tuple-element.299), channel_id=1, source_target_pairs={{28,0},{0,4},{4,8},{8,12},{12,16},{16,20},{20,24},{24,28},{29,1},{... | collective-permute-start | bytes 776 | tf_op jit(solution)/shard_map/while/body/eval_jaxpr/ppermute | solution.py:21
  118.6 6.4 %collective-permute-start.2 = (f32[1,64]{1,0:T(1,128)S(1)}, f32[1,64]{1,0:T(1,128)S(1)}, u32[]{:S(2)}, u32[]{:S(2)}) collective-permute-start(f32[1,64]{1,0:T(1,128)S(1)} %get-tuple-element.300), channel_id=1, source_target_pairs={{28,0},{0,4},{4,8},{8,12},{12,16},{16,20},{20,24},{24,28},{29,1},{... | collective-permute-start | bytes 776 | tf_op jit(solution)/shard_map/while/body/eval_jaxpr/ppermute | solution.py:21
  132.8 7.0 %collective-permute-start.3 = (f32[1,64,512]{2,1,0:T(8,128)S(1)}, f32[1,64,512]{2,1,0:T(8,128)}, u32[]{:S(2)}, u32[]{:S(2)}) collective-permute-start(f32[1,64,512]{2,1,0:T(8,128)S(1)} %fusion.112), channel_id=1, source_target_pairs={{28,0},{0,4},{4,8},{8,12},{12,16},{16,20},{20,24},{24,28},{29,1},{... | collective-permute-start | bytes 393224 | tf_op jit(solution)/shard_map/while/body/eval_jaxpr/ppermute | solution.py:21
  132.9 6.9 %collective-permute-start = (bf16[1,36864]{1,0:T(2,128)(2,1)S(1)}, bf16[1,36864]{1,0:T(2,128)(2,1)S(1)}, u32[]{:S(2)}, u32[]{:S(2)}) collective-permute-start(bf16[1,36864]{1,0:T(2,128)(2,1)S(1)} %copy.35), channel_id=1, source_target_pairs={{28,0},{0,4},{4,8},{8,12},{12,16},{16,20},{20,24},{24,28},{29,1},{... | collective-permute-start | bytes 221192 | tf_op jit(solution)/shard_map/while/body/eval_jaxpr/ppermute | solution.py:21
  133.0 6.8 %collective-permute-start.1 = (f32[1,64]{1,0:T(1,128)S(1)}, f32[1,64]{1,0:T(1,128)S(1)}, u32[]{:S(2)}, u32[]{:S(2)}) collective-permute-start(f32[1,64]{1,0:T(1,128)S(1)} %get-tuple-element.299), channel_id=1, source_target_pairs={{28,0},{0,4},{4,8},{8,12},{12,16},{16,20},{20,24},{24,28},{29,1},{... | collective-permute-start | bytes 776 | tf_op jit(solution)/shard_map/while/body/eval_jaxpr/ppermute | solution.py:21
  133.4 6.4 %collective-permute-start.2 = (f32[1,64]{1,0:T(1,128)S(1)}, f32[1,64]{1,0:T(1,128)S(1)}, u32[]{:S(2)}, u32[]{:S(2)}) collective-permute-start(f32[1,64]{1,0:T(1,128)S(1)} %get-tuple-element.300), channel_id=1, source_target_pairs={{28,0},{0,4},{4,8},{8,12},{12,16},{16,20},{20,24},{24,28},{29,1},{... | collective-permute-start | bytes 776 | tf_op jit(solution)/shard_map/while/body/eval_jaxpr/ppermute | solution.py:21
  146.1 8.6 %all-to-all-start = ((bf16[8,2,2048]{2,1,0:T(2,128)(2,1)}), bf16[8,2,2048]{2,1,0:T(2,128)(2,1)S(1)}, u32[]{:S(2)}, u32[]{:S(2)}) async-start(bf16[8,2,2048]{2,1,0:T(2,128)(2,1)} %reshape.378), calls=%async_computation | async-start | bytes 131072 | tf_op jit(solution)/shard_map/all_to_all | solution.py:137
  149.6 66.1 %all-reduce.3.cloned.1.call-start = ((), (), s32[]{:S(2)}) async-start(), calls=%async_computation.1 | async-start | bytes 229376
  (16 other events, 356.6 us)
Sparse Core Ops, SparseCore 0:
  164.3 51.3 all-reduce.2
where the time goes:
time: 225 us
  waiting for transfers between devices  79.8 us (35%)
  matrix products  68.6 us (30%)
  starting transfers between devices  36.3 us (16%)
  other arithmetic  16.6 us (7%)
  between operations  13.6 us (6%)
  local copies, waits for them, and re-layouts  9.15 us (4%)
    unnamed x2, waiting for transfers between devices  51 us
    ppermute x32, starting transfers between devices, passed_along(): return lax.ppermute(block, axis, route)  32.7 us
    dot_general x8, matrix products, prefix_part(): jnp.einsum('nhk,tk->nht', queries, prefix_cache, preferred_element_type=j...  28.8 us
    ppermute x32, waiting for transfers between devices, passed_along(): return lax.ppermute(block, axis, route)  23.9 us
    dot_general x8, matrix products, partial_softmax(): jnp.einsum('nht,tl->nhl', weights_low, values, preferred_element_type=jnp...  18.5 us
    dot_general x1, matrix products, on_device(): jnp.dot(head_out, out_weight, preferred_element_type=jnp.float32)  7.84 us
    broadcast_in_dim x8, other arithmetic, prefix_part(): jnp.broadcast_to((mask_rows > 0)[:, :, None], (count_rows, blocks_here, B...  5.6 us
    all_to_all x1, waiting for transfers between devices, on_device(): lax.all_to_all(context, 'blk', split_axis=1, concat_axis=0, tiled=True)  4.95 us
  transfers between devices with their start and end apart: 34, of which 10 were waited for; matrix products, arithmetic and copies ran while one was open for 0% of the time, Pallas kernels for 0%

commit v1 on v0

v1 whole, which is shorter than its diff:
```python
import functools
import math

import jax
import jax.numpy as jnp
from jax import lax
from jax.experimental import pallas as pl
from jax.experimental.pallas import tpu as pltpu
from jax.sharding import PartitionSpec as P

D = 7168
H = 64
LAT = 512
QK = 192
RANK = 16
BLOCK = 128
KV = 576
FLOOR = -1e30
CHUNK = 1024
GROUP = 4
PARTS = 8
SCALE = QK ** (-0.5) * math.log2(math.e)
F32 = jnp.float32
BF16 = jnp.bfloat16
NT = (((1,), (1,)), ((), ()))


def split3(x):
    hi = x.astype(BF16).astype(F32)
    rest = x - hi
    mid = rest.astype(BF16).astype(F32)
    return hi, mid, rest - mid


def attend_chunk(state, queries, keys, bias):
    peak, total, sums = state
    scores = lax.dot_general(queries, keys, NT, preferred_element_type=F32) * SCALE + bias
    fresh = jnp.maximum(peak, jnp.max(scores, axis=1, keepdims=True))
    weights = jnp.exp2(scores - fresh)
    keep = jnp.exp2(peak - fresh)
    total = total * keep + jnp.sum(weights, axis=1, keepdims=True)
    sums = sums * keep + jnp.dot(weights.astype(BF16), keys[:, :LAT], preferred_element_type=F32)
    return fresh, total, sums


def kernel(
    n,
    tenant_ref, length_ref,
    base_ref, latent_ref, qa_hbm, qb_hbm, prefix_hbm, mask_ref, suffix_hbm, new_ref,
    up_hbm, weight_hbm, oa_hbm, ob_hbm,
    out_ref,
    qa, qb, prefix, suffix, up, weight, oa, ob,
    pair_scr, head_scr, queries, bias_scr, sums_scr, stat_scr, send, recv, ctx_scr, row_scr, out_send, out_recv,
    load_sem, q_send, q_recv, p_send, p_recv, o_send, o_recv,
):
    me = lax.axis_index("blk")
    bits = n.bit_length() - 1
    heads_here = H // n

    def peer(k):
        total = 0
        for b in range(bits):
            total = total + lax.rem(lax.div(me, 1 << b) + (k >> b & 1), 2) * (1 << b)
        return total

    peers = [peer(k) for k in range(n)]
    loads = [
        pltpu.make_async_copy(src, dst, load_sem.at[i])
        for i, (src, dst) in enumerate(
            [(qa_hbm, qa), (qb_hbm, qb), (suffix_hbm.at[0], suffix), (prefix_hbm, prefix),
             (up_hbm, up), (oa_hbm, oa), (ob_hbm, ob), (weight_hbm, weight)]
        )
    ]
    for load in loads:
        load.start()

    barrier = pltpu.get_barrier_semaphore()
    for k in range(1, n):
        pl.semaphore_signal(barrier, inc=1, device_id={"blk": peers[k]}, device_id_type=pl.DeviceIdType.MESH)

    loads[0].wait()
    own_tenant = tenant_ref[me]
    latent = jnp.broadcast_to(latent_ref[...].astype(F32), (16, latent_ref.shape[1])).astype(BF16)
    tenants = qa.shape[0]
    lows = []
    for t in range(tenants):
        low = jnp.dot(latent, qa[t], preferred_element_type=F32)
        lows.append(jnp.where(own_tenant == t, low, 0.0))
    low_spread = jnp.concatenate(lows, axis=1).astype(BF16)
    loads[1].wait()
    row_id = lax.broadcasted_iota(jnp.int32, (8, 2 * KV), 0)
    for i in range(H // 16):
        columns = slice(i * 16 * KV, (i + 1) * 16 * KV)
        up_map = qb[:, :, columns].reshape(tenants * RANK, 16 * KV)
        delta = jnp.dot(low_spread, up_map, preferred_element_type=F32)[:8]
        full = delta + base_ref[:, columns].astype(F32)
        rows = full[:, : 2 * KV]
        for p in range(1, 8):
            rows = jnp.where(row_id == p, full[:, p * 2 * KV : (p + 1) * 2 * KV], rows)
        pair_scr[i * 8 : (i + 1) * 8, :] = rows
    even = pair_scr[:, :KV]
    odd = pair_scr[:, KV:]
    tiles = [(lt, min(128, KV - lt * 128)) for lt in range(pl.cdiv(KV, 128))]
    for lt, width in tiles:
        head_scr[lt, pl.ds(0, H // 2, stride=2), :width] = even[:, lt * 128 : lt * 128 + width]
        head_scr[lt, pl.ds(1, H // 2, stride=2), :width] = odd[:, lt * 128 : lt * 128 + width]
    for lt, width in tiles:
        queries[0, :, lt * 128 : lt * 128 + width] = head_scr[lt, :, :width].astype(BF16)

    pl.semaphore_wait(barrier, n - 1)
    q_copies = []
    for k in range(1, n):
        copy = pltpu.make_async_remote_copy(
            src_ref=queries.at[0], dst_ref=queries.at[k], send_sem=q_send.at[k], recv_sem=q_recv.at[k],
            device_id={"blk": peers[k]}, device_id_type=pl.DeviceIdType.MESH)
        copy.start()
        q_copies.append(copy)

    live = jnp.where(mask_ref[...] > 0, 0.0, -jnp.inf).astype(F32)
    for b in range(mask_ref.shape[1]):
        bias_scr[:, b * BLOCK : (b + 1) * BLOCK] = jnp.broadcast_to(live[:, b : b + 1], (n, BLOCK))

    own = queries[0]
    fresh_key = new_ref[...].astype(F32)
    new_score = jnp.sum(own.astype(F32) * fresh_key, axis=1, keepdims=True) * SCALE
    state = (new_score, jnp.ones((H, 1), F32), jnp.broadcast_to(fresh_key[:, :LAT], (H, LAT)))
    length = length_ref[0, lax.axis_index("batch")] * BLOCK
    loads[2].wait()

    def suffix_step(c, state):
        start = pl.multiple_of(c * CHUNK, CHUNK)
        token = lax.broadcasted_iota(jnp.int32, (1, CHUNK), 1) + start
        bias = jnp.where(token < length, 0.0, -jnp.inf).astype(F32)
        return attend_chunk(state, own, suffix[pl.ds(start, CHUNK), :], bias)

    own_state = lax.fori_loop(0, suffix.shape[0] // CHUNK, suffix_step, state)
    loads[3].wait()

    rows = GROUP * H
    p_copies = []
    lane = lax.broadcasted_iota(jnp.int32, (rows, 128), 1)
    for g in range(n // GROUP):
        for j in range(GROUP):
            if g * GROUP + j > 0:
                q_copies[g * GROUP + j - 1].wait_recv()
        if g == 0:
            fill = rows - H
            start_state = (
                jnp.concatenate([own_state[0], jnp.full((fill, 1), FLOOR, F32)], axis=0),
                jnp.concatenate([own_state[1], jnp.zeros((fill, 1), F32)], axis=0),
                jnp.concatenate([own_state[2], jnp.zeros((fill, LAT), F32)], axis=0),
            )
        else:
            start_state = (jnp.full((rows, 1), FLOOR, F32), jnp.zeros((rows, 1), F32), jnp.zeros((rows, LAT), F32))
        group_queries = queries[g * GROUP : (g + 1) * GROUP].reshape(rows, KV)

        def prefix_step(c, state, g=g, group_queries=group_queries):
            start = pl.multiple_of(c * CHUNK, CHUNK)
            bias = jnp.concatenate(
                [jnp.broadcast_to(bias_scr[pl.ds(peers[g * GROUP + j], 1), pl.ds(start, CHUNK)], (H, CHUNK))
                 for j in range(GROUP)], axis=0)
            return attend_chunk(state, group_queries, prefix[pl.ds(start, CHUNK), :], bias)

        peak, total, sums = lax.fori_loop(0, prefix.shape[0] // CHUNK, prefix_step, start_state)
        stats = jnp.zeros((rows, 128), F32)
        for i, piece in enumerate(split3(peak) + split3(total)):
            stats = jnp.where(lane == i, piece, stats)
        span = slice(g * GROUP * heads_here, (g + 1) * GROUP * heads_here)
        for d in range(n):
            pick = [slice(j * H + d * heads_here, j * H + (d + 1) * heads_here) for j in range(GROUP)]
            send[d, span, :LAT] = jnp.concatenate([sums[s] for s in pick], axis=0).astype(BF16)
            send[d, span, LAT:] = jnp.concatenate([stats[s] for s in pick], axis=0).astype(BF16)
        for k in range(1, n):
            copy = pltpu.make_async_remote_copy(
                src_ref=send.at[peers[k], span], dst_ref=recv.at[k, span],
                send_sem=p_send.at[g, k], recv_sem=p_recv.at[g, k],
                device_id={"blk": peers[k]}, device_id_type=pl.DeviceIdType.MESH)
            copy.start()
            p_copies.append(copy)

    recv[0] = send[me]
    for copy in p_copies:
        copy.wait_recv()

    for q in range(n):
        parts = []
        for k in range(n):
            j = k ^ q
            block = recv[k, j * heads_here : (j + 1) * heads_here, :].astype(F32)
            stats = block[:, LAT:]
            m = stats[:, 0:1] + stats[:, 1:2] + stats[:, 2:3]
            l = stats[:, 3:4] + stats[:, 4:5] + stats[:, 5:6]
            parts.append((m, l, block[:, :LAT]))
        peak = functools.reduce(jnp.maximum, [p[0] for p in parts])
        total = jnp.zeros_like(peak)
        sums = jnp.zeros((heads_here, LAT), F32)
        for m, l, s in parts:
            w = jnp.exp2(m - peak)
            total = total + w * l
            sums = sums + w * s
        context = sums / total
        for lt in range(LAT // 128):
            ctx_scr[lt, q * heads_here : (q + 1) * heads_here, :] = context[:, lt * 128 : (lt + 1) * 128]

    for i in (4, 5, 6, 7):
        loads[i].wait()
    outs = []
    for h in range(heads_here):
        rows_h = jnp.concatenate(
            [ctx_scr[lt, pl.ds(h, n, stride=heads_here), :] for lt in range(LAT // 128)], axis=1)
        outs.append(jnp.dot(rows_h.astype(BF16), up[h], preferred_element_type=F32))
    head_out = jnp.concatenate(outs, axis=1).astype(BF16)
    request = lax.broadcasted_iota(jnp.int32, (n, RANK), 0)
    tenant_of = jnp.zeros((n, RANK), jnp.int32)
    for q in range(n):
        tenant_of = jnp.where(request == q, tenant_ref[peers[q]], tenant_of)
    lows = []
    for t in range(tenants):
        low = jnp.dot(head_out, oa[t], preferred_element_type=F32)
        lows.append(jnp.where(tenant_of == t, low, 0.0))
    low_out = jnp.concatenate(split3(jnp.concatenate(lows, axis=1)), axis=0).astype(BF16)
    adapter_up = ob[...].reshape(tenants * RANK, D)
    width = D // PARTS
    for c in range(PARTS // 2):
        columns = slice(c * 2 * width, (c + 1) * 2 * width)
        projected = jnp.dot(head_out, weight[:, columns], preferred_element_type=F32)
        added = jnp.dot(low_out, adapter_up[:, columns], preferred_element_type=F32)
        projected = projected + (added[:n] + added[n : 2 * n] + added[2 * n :])
        for half in range(2):
            for lt in range(width // 128):
                row_scr[lt, (2 * c + half) * n : (2 * c + half + 1) * n, :] = projected[
                    :, half * width + lt * 128 : half * width + (lt + 1) * 128]
    o_copies = []
    for q in list(range(1, n)) + [0]:
        target = out_recv if q == 0 else out_send
        for lt in range(width // 128):
            target[q, :, lt * 128 : (lt + 1) * 128] = row_scr[lt, pl.ds(q, PARTS, stride=n), :].astype(BF16)
        if q:
            copy = pltpu.make_async_remote_copy(
                src_ref=out_send.at[q], dst_ref=out_recv.at[q], send_sem=o_send.at[q], recv_sem=o_recv.at[q],
                device_id={"blk": peers[q]}, device_id_type=pl.DeviceIdType.MESH)
            copy.start()
            o_copies.append(copy)
    result = out_recv[0].astype(F32)
    for q in range(1, n):
        o_copies[q - 1].wait_recv()
        result = result + out_recv[q].astype(F32)
    out_ref[...] = result.astype(BF16)
    for copy in q_copies + p_copies + o_copies:
        copy.wait_send()


def on_device(
    query_base, query_latent, tenant_ids, adapter_qa, adapter_qb, prefix_cache, prefix_mask, suffix_cache,
    suffix_blocks, new_latent, value_up, out_weight, adapter_oa, adapter_ob,
):
    n = lax.axis_size("blk")
    vmem = pl.BlockSpec(memory_space=pltpu.VMEM)
    smem = pl.BlockSpec(memory_space=pltpu.SMEM)
    hbm = pl.BlockSpec(memory_space=pl.ANY)
    dma = pltpu.SemaphoreType.DMA
    slots = prefix_cache.shape[0]
    heads_here = H // n
    out = pl.pallas_call(
        functools.partial(kernel, n),
        out_shape=jax.ShapeDtypeStruct((PARTS, D // PARTS), BF16),
        in_specs=[smem, smem, vmem, vmem, hbm, hbm, hbm, vmem, hbm, vmem, hbm, hbm, hbm, hbm],
        out_specs=vmem,
        scratch_shapes=[
            pltpu.VMEM(adapter_qa.shape, BF16),
            pltpu.VMEM(adapter_qb.shape, BF16),
            pltpu.VMEM(prefix_cache.shape, BF16),
            pltpu.VMEM(suffix_cache.shape[1:], BF16),
            pltpu.VMEM(value_up.shape, BF16),
            pltpu.VMEM(out_weight.shape, BF16),
            pltpu.VMEM(adapter_oa.shape, BF16),
            pltpu.VMEM(adapter_ob.shape, BF16),
            pltpu.VMEM((H // 2, 2 * KV), F32),
            pltpu.VMEM((pl.cdiv(KV, 128), H, 128), F32),
            pltpu.VMEM((n, H, KV), BF16),
            pltpu.VMEM((n, slots), F32),
            pltpu.VMEM((8, 128), F32),
            pltpu.VMEM((8, 128), F32),
            pltpu.VMEM((n, n * heads_here, LAT + 128), BF16),
            pltpu.VMEM((n, n * heads_here, LAT + 128), BF16),
            pltpu.VMEM((LAT // 128, n * heads_here, 128), F32),
            pltpu.VMEM((D // PARTS // 128, PARTS * n, 128), F32),
            pltpu.VMEM((n, PARTS, D // PARTS), BF16),
            pltpu.VMEM((n, PARTS, D // PARTS), BF16),
            dma((8,)), dma((n,)), dma((n,)), dma((n // GROUP, n)), dma((n // GROUP, n)), dma((n,)), dma((n,)),
        ],
        compiler_params=pltpu.CompilerParams(
            collective_id=0, has_side_effects=True, vmem_limit_bytes=60 << 20),
    )(
        tenant_ids, suffix_blocks, query_base, query_latent, adapter_qa, adapter_qb, prefix_cache, prefix_mask,
        suffix_cache, new_latent, value_up, out_weight, adapter_oa, adapter_ob,
    )
    return out.reshape(1, D)


def solution(mesh):
    placed = (
        P(("batch", "blk"), None),
        P(("batch", "blk"), None),
        P("batch"),
        P(),
        P(),
        P("blk", None),
        P("batch", "blk"),
        P(("batch", "blk"), None, None),
        P("blk", None),
        P(("batch", "blk"), None),
        P("blk", None, None),
        P("blk", None),
        P(None, "blk", None),
        P(),
    )
    return jax.shard_map(
        on_device, mesh=mesh, in_specs=placed, out_specs=P(("batch", "blk"), None), check_vma=False
    )
```

time: 225 us -> 57.8 us (0.26)
  waiting for transfers between devices: 79.8 us -> 0 us
  matrix products: 68.6 us -> 0 us
  starting transfers between devices: 36.3 us -> 0 us
  Pallas kernels: 0 us -> 36 us
  other arithmetic: 16.6 us -> 0 us
  between operations: 13.6 us -> 0.01 us
  local copies, waits for them, and re-layouts: 9.15 us -> 21.2 us
    dot_general x25 -> x0, matrix products: 68.6 us -> none  [the longest x8 28.8 us: prefix_part(): jnp.einsum('nhk,tk->nht', queries, prefix_cache, preferred_element_type=j...]
    unnamed x2 -> x0, waiting for transfers between devices: 51 us -> none
    pallas_call x0 -> x1, Pallas kernels: none -> 36 us  [on_device(): pl.pallas_call(functools.partial(kernel, n), out_shape=jax.ShapeDtypeStru...]
    ppermute x32 -> x0, starting transfers between devices: 32.7 us -> none  [passed_along(): return lax.ppermute(block, axis, route)]
    ppermute x32 -> x0, waiting for transfers between devices: 23.9 us -> none  [passed_along(): return lax.ppermute(block, axis, route)]
    unnamed x18 -> x5, local copies, waits for them, and re-layouts: 3.96 us -> 21.2 us
    broadcast_in_dim x8 -> x0, other arithmetic: 5.6 us -> none  [prefix_part(): jnp.broadcast_to((mask_rows > 0)[:, :, None], (count_rows, blocks_here, B...]
    all_to_all x1 -> x0, waiting for transfers between devices: 4.95 us -> none  [on_device(): lax.all_to_all(context, 'blk', split_axis=1, concat_axis=0, tiled=True)]
  transfers between devices with their start and end apart: 34 -> 0, of which waited for: 10 -> 0; matrix products, arithmetic and copies ran while one was open for 0% -> 0% of each run, Pallas kernels for 0% -> 0%
where the time goes in v1:
time: 57.8 us; the launch traced here: 57.2 us
  Pallas kernels  36 us (62%)
  local copies, waits for them, and re-layouts  21.2 us (37%)
    pallas_call x1, Pallas kernels, on_device(): pl.pallas_call(functools.partial(kernel, n), out_shape=jax.ShapeDtypeStru...  36 us
    unnamed x5, local copies, waits for them, and re-layouts  21.2 us

profile of v1, /device:TPU:0, one launch (start us, length us, event | category | flops | bytes accessed | tf_op | source)
XLA Modules:
  0.0 57.2 jit_solution(7070303501862254463)
XLA Ops:
  0.0 2.2 %copy.18.oa_hbm = bf16[4,1024,16]{2,1,0:T(8,128)(2,1)} copy(bf16[4,1024,16]{1,2,0:T(8,128)(2,1)} %param.26) | data formatting | bytes 262144 | tf_op args[12]
  2.2 2.3 %copy.15.qa_hbm = bf16[4,1536,16]{2,1,0:T(8,128)(2,1)} copy(bf16[4,1536,16]{1,2,0:T(8,128)(2,1)} %param.17) | data formatting | bytes 393216 | tf_op args[3]
  4.6 7.6 %copy.16.prefix_hbm = bf16[4096,576]{1,0:T(8,128)(2,1)} copy(bf16[4096,576]{0,1:T(8,128)(2,1)} %param.19) | data formatting | bytes 9437184 | tf_op args[5]
  12.2 7.6 %copy.17.suffix_hbm = bf16[1,4096,576]{2,1,0:T(8,128)(2,1)} copy(bf16[1,4096,576]{1,2,0:T(8,128)(2,1)} %param.21) | data formatting | bytes 9437184 | tf_op args[7]
  19.8 36.0 %shard_map.136 = bf16[8,896]{1,0:T(8,128)(2,1)} custom-call(s32[8]{0:T(128)} %tenant_ref.1, s32[1,4]{1,0:T(1,128)} %length_ref.1, bf16[1,36864]{1,0:T(2,128)(2,1)} %base_ref.1, bf16[1,1536]{1,0:T(2,128)(2,1)} %latent_ref.1, bf16[4,1536,16]{2,1,0:T(8,128)(2,1)} %copy.15.qa_hbm, bf16[4,16,36864]{2,1,0:T(8,128)(2,1)} %qb_hbm.1, ...), custom_call_target="tpu_custom_call" | custom-call | tf_op jit(solution)/shard_map/pallas_call | solution.py:264
  55.9 1.3 %copy.19 = bf16[1,1,8,896]{3,1,2,0:T(2,128)(2,1)} copy(bf16[1,1,8,896]{3,2,1,0:T(8,128)(2,1)} %bitcast.3) | data formatting | bytes 28672

commit v2 on v1

--- a/solution.py
+++ b/solution.py
@@ -34,12 +34,13 @@
 
 def attend_chunk(state, queries, keys, bias):
     peak, total, sums = state
-    scores = lax.dot_general(queries, keys, NT, preferred_element_type=F32) * SCALE + bias
+    scores = jnp.dot(queries, keys, preferred_element_type=F32) * SCALE + bias
     fresh = jnp.maximum(peak, jnp.max(scores, axis=1, keepdims=True))
     weights = jnp.exp2(scores - fresh)
     keep = jnp.exp2(peak - fresh)
     total = total * keep + jnp.sum(weights, axis=1, keepdims=True)
-    sums = sums * keep + jnp.dot(weights.astype(BF16), keys[:, :LAT], preferred_element_type=F32)
+    sums = sums * keep + lax.dot_general(
+        weights.astype(BF16), keys[:LAT], NT, preferred_element_type=F32)
     return fresh, total, sums
 
 
@@ -50,7 +51,7 @@
     up_hbm, weight_hbm, oa_hbm, ob_hbm,
     out_ref,
     qa, qb, prefix, suffix, up, weight, oa, ob,
-    pair_scr, head_scr, queries, bias_scr, sums_scr, stat_scr, send, recv, ctx_scr, row_scr, out_send, out_recv,
+    pair_scr, head_scr, queries, bias_scr, send, recv, ctx_scr, row_scr, out_send, out_recv,
     load_sem, q_send, q_recv, p_send, p_recv, o_send, o_recv,
 ):
     me = lax.axis_index("blk")
@@ -84,7 +85,7 @@
     tenants = qa.shape[0]
     lows = []
     for t in range(tenants):
-        low = jnp.dot(latent, qa[t], preferred_element_type=F32)
+        low = lax.dot_general(latent, qa[t], NT, preferred_element_type=F32)
         lows.append(jnp.where(own_tenant == t, low, 0.0))
     low_spread = jnp.concatenate(lows, axis=1).astype(BF16)
     loads[1].wait()
@@ -131,9 +132,9 @@
         start = pl.multiple_of(c * CHUNK, CHUNK)
         token = lax.broadcasted_iota(jnp.int32, (1, CHUNK), 1) + start
         bias = jnp.where(token < length, 0.0, -jnp.inf).astype(F32)
-        return attend_chunk(state, own, suffix[pl.ds(start, CHUNK), :], bias)
-
-    own_state = lax.fori_loop(0, suffix.shape[0] // CHUNK, suffix_step, state)
+        return attend_chunk(state, own, suffix[:, pl.ds(start, CHUNK)], bias)
+
+    own_state = lax.fori_loop(0, suffix.shape[1] // CHUNK, suffix_step, state)
     loads[3].wait()
 
     rows = GROUP * H
@@ -159,9 +160,9 @@
             bias = jnp.concatenate(
                 [jnp.broadcast_to(bias_scr[pl.ds(peers[g * GROUP + j], 1), pl.ds(start, CHUNK)], (H, CHUNK))
                  for j in range(GROUP)], axis=0)
-            return attend_chunk(state, group_queries, prefix[pl.ds(start, CHUNK), :], bias)
-
-        peak, total, sums = lax.fori_loop(0, prefix.shape[0] // CHUNK, prefix_step, start_state)
+            return attend_chunk(state, group_queries, prefix[:, pl.ds(start, CHUNK)], bias)
+
+        peak, total, sums = lax.fori_loop(0, prefix.shape[1] // CHUNK, prefix_step, start_state)
         stats = jnp.zeros((rows, 128), F32)
         for i, piece in enumerate(split3(peak) + split3(total)):
             stats = jnp.where(lane == i, piece, stats)
@@ -216,7 +217,7 @@
         tenant_of = jnp.where(request == q, tenant_ref[peers[q]], tenant_of)
     lows = []
     for t in range(tenants):
-        low = jnp.dot(head_out, oa[t], preferred_element_type=F32)
+        low = lax.dot_general(head_out, oa[t], NT, preferred_element_type=F32)
         lows.append(jnp.where(tenant_of == t, low, 0.0))
     low_out = jnp.concatenate(split3(jnp.concatenate(lows, axis=1)), axis=0).astype(BF16)
     adapter_up = ob[...].reshape(tenants * RANK, D)
@@ -255,11 +256,15 @@
     suffix_blocks, new_latent, value_up, out_weight, adapter_oa, adapter_ob,
 ):
     n = lax.axis_size("blk")
+    prefix_cache = prefix_cache.T
+    suffix_cache = suffix_cache.transpose(0, 2, 1)
+    adapter_qa = adapter_qa.transpose(0, 2, 1)
+    adapter_oa = adapter_oa.transpose(0, 2, 1)
     vmem = pl.BlockSpec(memory_space=pltpu.VMEM)
     smem = pl.BlockSpec(memory_space=pltpu.SMEM)
     hbm = pl.BlockSpec(memory_space=pl.ANY)
     dma = pltpu.SemaphoreType.DMA
-    slots = prefix_cache.shape[0]
+    slots = prefix_cache.shape[1]
     heads_here = H // n
     out = pl.pallas_call(
         functools.partial(kernel, n),
@@ -279,8 +284,6 @@
             pltpu.VMEM((pl.cdiv(KV, 128), H, 128), F32),
             pltpu.VMEM((n, H, KV), BF16),
             pltpu.VMEM((n, slots), F32),
-            pltpu.VMEM((8, 128), F32),
-            pltpu.VMEM((8, 128), F32),
             pltpu.VMEM((n, n * heads_here, LAT + 128), BF16),
             pltpu.VMEM((n, n * heads_here, LAT + 128), BF16),
             pltpu.VMEM((LAT // 128, n * heads_here, 128), F32),

time: 57.8 us -> 36.9 us (0.64)
  local copies, waits for them, and re-layouts: 21.2 us -> 1.34 us
  Pallas kernels: 36 us -> 35.3 us
    unnamed x5 -> x1, local copies, waits for them, and re-layouts: 21.2 us -> 1.34 us
    pallas_call x1, Pallas kernels: 36 us -> 35.3 us  [on_device(): pl.pallas_call(functools.partial(kernel, n), out_shape=jax.ShapeDtypeStru...]
where the time goes in v2:
time: 36.9 us; the launch traced here: 36.6 us
  Pallas kernels  35.3 us (96%)
  local copies, waits for them, and re-layouts  1.34 us (4%)
    pallas_call x1, Pallas kernels, on_device(): pl.pallas_call(functools.partial(kernel, n), out_shape=jax.ShapeDtypeStru...  35.3 us
    unnamed x1, local copies, waits for them, and re-layouts  1.34 us

profile of v2, /device:TPU:0, one launch (start us, length us, event | category | flops | bytes accessed | tf_op | source)
XLA Modules:
  0.0 36.6 jit_solution(12262844015462881326)
XLA Ops:
  0.0 35.3 %shard_map.136 = bf16[8,896]{1,0:T(8,128)(2,1)} custom-call(s32[8]{0:T(128)} %tenant_ref.1, s32[1,4]{1,0:T(1,128)} %length_ref.1, bf16[1,36864]{1,0:T(2,128)(2,1)} %base_ref.1, bf16[1,1536]{1,0:T(2,128)(2,1)} %latent_ref.1, bf16[4,16,1536]{2,1,0:T(8,128)(2,1)} %bitcast.9, bf16[4,16,36864]{2,1,0:T(8,128)(2,1)} %qb_hbm.1, bf16[576,4096]{1,0:T(8,128)(2,1)} %bitcast.7, ...), custom_call_target="tpu_custom_call" | custom-call | tf_op jit(solution)/shard_map/pallas_call | solution.py:269
  35.3 1.3 %copy.15 = bf16[1,1,8,896]{3,1,2,0:T(2,128)(2,1)} copy(bf16[1,1,8,896]{3,2,1,0:T(8,128)(2,1)} %bitcast.11) | data formatting | bytes 28672

commit v3 on v2

--- a/solution.py
+++ b/solution.py
@@ -16,7 +16,7 @@
 BLOCK = 128
 KV = 576
 FLOOR = -1e30
-CHUNK = 1024
+CHUNK = 2048
 GROUP = 4
 PARTS = 8
 SCALE = QK ** (-0.5) * math.log2(math.e)
@@ -52,7 +52,7 @@
     out_ref,
     qa, qb, prefix, suffix, up, weight, oa, ob,
     pair_scr, head_scr, queries, bias_scr, send, recv, ctx_scr, row_scr, out_send, out_recv,
-    load_sem, q_send, q_recv, p_send, p_recv, o_send, o_recv,
+    early_sem, load_sem, q_send, q_recv, p_send, p_recv, o_send, o_recv,
 ):
     me = lax.axis_index("blk")
     bits = n.bit_length() - 1
@@ -65,33 +65,39 @@
         return total
 
     peers = [peer(k) for k in range(n)]
+    span_q = qb.shape[2] // 4
+    early = [pltpu.make_async_copy(qa_hbm, qa, early_sem.at[4])] + [
+        pltpu.make_async_copy(
+            qb_hbm.at[:, :, i * span_q : (i + 1) * span_q], qb.at[:, :, i * span_q : (i + 1) * span_q], early_sem.at[i])
+        for i in range(4)
+    ]
     loads = [
         pltpu.make_async_copy(src, dst, load_sem.at[i])
         for i, (src, dst) in enumerate(
-            [(qa_hbm, qa), (qb_hbm, qb), (suffix_hbm.at[0], suffix), (prefix_hbm, prefix),
+            [(suffix_hbm.at[0], suffix), (prefix_hbm, prefix),
              (up_hbm, up), (oa_hbm, oa), (ob_hbm, ob), (weight_hbm, weight)]
         )
     ]
-    for load in loads:
+    for load in early:
         load.start()
 
     barrier = pltpu.get_barrier_semaphore()
     for k in range(1, n):
         pl.semaphore_signal(barrier, inc=1, device_id={"blk": peers[k]}, device_id_type=pl.DeviceIdType.MESH)
 
-    loads[0].wait()
+    early[0].wait()
     own_tenant = tenant_ref[me]
     latent = jnp.broadcast_to(latent_ref[...].astype(F32), (16, latent_ref.shape[1])).astype(BF16)
     tenants = qa.shape[0]
-    lows = []
-    for t in range(tenants):
-        low = lax.dot_general(latent, qa[t], NT, preferred_element_type=F32)
-        lows.append(jnp.where(own_tenant == t, low, 0.0))
-    low_spread = jnp.concatenate(lows, axis=1).astype(BF16)
-    loads[1].wait()
+    lane_tenant = lax.broadcasted_iota(jnp.int32, (16, tenants * RANK), 1) // RANK
+    low = lax.dot_general(latent, qa[...].reshape(tenants * RANK, qa.shape[2]), NT, preferred_element_type=F32)
+    low_spread = jnp.where(lane_tenant == own_tenant, low, 0.0).astype(BF16)
     row_id = lax.broadcasted_iota(jnp.int32, (8, 2 * KV), 0)
     for i in range(H // 16):
         columns = slice(i * 16 * KV, (i + 1) * 16 * KV)
+        early[i + 1].wait()
+        if i >= 2:
+            loads[i - 2].start()
         up_map = qb[:, :, columns].reshape(tenants * RANK, 16 * KV)
         delta = jnp.dot(low_spread, up_map, preferred_element_type=F32)[:8]
         full = delta + base_ref[:, columns].astype(F32)
@@ -109,13 +115,26 @@
         queries[0, :, lt * 128 : lt * 128 + width] = head_scr[lt, :, :width].astype(BF16)
 
     pl.semaphore_wait(barrier, n - 1)
-    q_copies = []
-    for k in range(1, n):
+    order = [0, 1] + list(range(2, n, 2)) + list(range(3, n, 2))
+    place = [order.index(k) for k in range(n)]
+    q_copies = {}
+
+    def send_query(source, target, to):
         copy = pltpu.make_async_remote_copy(
-            src_ref=queries.at[0], dst_ref=queries.at[k], send_sem=q_send.at[k], recv_sem=q_recv.at[k],
-            device_id={"blk": peers[k]}, device_id_type=pl.DeviceIdType.MESH)
+            src_ref=queries.at[place[source]], dst_ref=queries.at[place[target]],
+            send_sem=q_send.at[target], recv_sem=q_recv.at[target],
+            device_id={"blk": peers[to]}, device_id_type=pl.DeviceIdType.MESH)
         copy.start()
-        q_copies.append(copy)
+        q_copies[target] = copy
+
+    def forward(k):
+        q_copies[k].wait_recv()
+        send_query(k, k + 1, 1)
+
+    for k in list(range(2, n, 2)) + [1]:
+        send_query(0, k, k)
+    for load in loads[2:]:
+        load.start()
 
     live = jnp.where(mask_ref[...] > 0, 0.0, -jnp.inf).astype(F32)
     for b in range(mask_ref.shape[1]):
@@ -126,7 +145,7 @@
     new_score = jnp.sum(own.astype(F32) * fresh_key, axis=1, keepdims=True) * SCALE
     state = (new_score, jnp.ones((H, 1), F32), jnp.broadcast_to(fresh_key[:, :LAT], (H, LAT)))
     length = length_ref[0, lax.axis_index("batch")] * BLOCK
-    loads[2].wait()
+    loads[0].wait()
 
     def suffix_step(c, state):
         start = pl.multiple_of(c * CHUNK, CHUNK)
@@ -134,16 +153,19 @@
         bias = jnp.where(token < length, 0.0, -jnp.inf).astype(F32)
         return attend_chunk(state, own, suffix[:, pl.ds(start, CHUNK)], bias)
 
-    own_state = lax.fori_loop(0, suffix.shape[1] // CHUNK, suffix_step, state)
-    loads[3].wait()
+    own_state = lax.fori_loop(0, suffix.shape[1] // CHUNK, suffix_step, state, unroll=True)
+    loads[1].wait()
 
     rows = GROUP * H
     p_copies = []
     lane = lax.broadcasted_iota(jnp.int32, (rows, 128), 1)
     for g in range(n // GROUP):
-        for j in range(GROUP):
-            if g * GROUP + j > 0:
-                q_copies[g * GROUP + j - 1].wait_recv()
+        members = order[g * GROUP : (g + 1) * GROUP]
+        for j in members:
+            if g == 0 and j >= 2:
+                forward(j)
+            elif j % 2:
+                q_copies[j].wait_recv()
         if g == 0:
             fill = rows - H
             start_state = (
@@ -155,14 +177,22 @@
             start_state = (jnp.full((rows, 1), FLOOR, F32), jnp.zeros((rows, 1), F32), jnp.zeros((rows, LAT), F32))
         group_queries = queries[g * GROUP : (g + 1) * GROUP].reshape(rows, KV)
 
-        def prefix_step(c, state, g=g, group_queries=group_queries):
+        def prefix_step(c, state, members=members, group_queries=group_queries):
             start = pl.multiple_of(c * CHUNK, CHUNK)
             bias = jnp.concatenate(
-                [jnp.broadcast_to(bias_scr[pl.ds(peers[g * GROUP + j], 1), pl.ds(start, CHUNK)], (H, CHUNK))
-                 for j in range(GROUP)], axis=0)
+                [jnp.broadcast_to(bias_scr[pl.ds(peers[j], 1), pl.ds(start, CHUNK)], (H, CHUNK))
+                 for j in members], axis=0)
             return attend_chunk(state, group_queries, prefix[:, pl.ds(start, CHUNK)], bias)
 
-        peak, total, sums = lax.fori_loop(0, prefix.shape[1] // CHUNK, prefix_step, start_state)
+        chunks = prefix.shape[1] // CHUNK
+        middle = 0
+        if g == 0:
+            middle = chunks // 2
+            start_state = lax.fori_loop(0, middle, prefix_step, start_state, unroll=True)
+            for j in order[GROUP:]:
+                if j % 2 == 0:
+                    forward(j)
+        peak, total, sums = lax.fori_loop(middle, chunks, prefix_step, start_state, unroll=True)
         stats = jnp.zeros((rows, 128), F32)
         for i, piece in enumerate(split3(peak) + split3(total)):
             stats = jnp.where(lane == i, piece, stats)
@@ -171,7 +201,7 @@
             pick = [slice(j * H + d * heads_here, j * H + (d + 1) * heads_here) for j in range(GROUP)]
             send[d, span, :LAT] = jnp.concatenate([sums[s] for s in pick], axis=0).astype(BF16)
             send[d, span, LAT:] = jnp.concatenate([stats[s] for s in pick], axis=0).astype(BF16)
-        for k in range(1, n):
+        for k in [k for k in order[::-1] if k > 1] + [1]:
             copy = pltpu.make_async_remote_copy(
                 src_ref=send.at[peers[k], span], dst_ref=recv.at[k, span],
                 send_sem=p_send.at[g, k], recv_sem=p_recv.at[g, k],
@@ -186,7 +216,7 @@
     for q in range(n):
         parts = []
         for k in range(n):
-            j = k ^ q
+            j = place[k ^ q]
             block = recv[k, j * heads_here : (j + 1) * heads_here, :].astype(F32)
             stats = block[:, LAT:]
             m = stats[:, 0:1] + stats[:, 1:2] + stats[:, 2:3]
@@ -203,7 +233,7 @@
         for lt in range(LAT // 128):
             ctx_scr[lt, q * heads_here : (q + 1) * heads_here, :] = context[:, lt * 128 : (lt + 1) * 128]
 
-    for i in (4, 5, 6, 7):
+    for i in (2, 3, 4, 5):
         loads[i].wait()
     outs = []
     for h in range(heads_here):
@@ -211,15 +241,14 @@
             [ctx_scr[lt, pl.ds(h, n, stride=heads_here), :] for lt in range(LAT // 128)], axis=1)
         outs.append(jnp.dot(rows_h.astype(BF16), up[h], preferred_element_type=F32))
     head_out = jnp.concatenate(outs, axis=1).astype(BF16)
-    request = lax.broadcasted_iota(jnp.int32, (n, RANK), 0)
-    tenant_of = jnp.zeros((n, RANK), jnp.int32)
+    request = lax.broadcasted_iota(jnp.int32, (n, tenants * RANK), 0)
+    tenant_of = jnp.zeros((n, tenants * RANK), jnp.int32)
     for q in range(n):
         tenant_of = jnp.where(request == q, tenant_ref[peers[q]], tenant_of)
-    lows = []
-    for t in range(tenants):
-        low = lax.dot_general(head_out, oa[t], NT, preferred_element_type=F32)
-        lows.append(jnp.where(tenant_of == t, low, 0.0))
-    low_out = jnp.concatenate(split3(jnp.concatenate(lows, axis=1)), axis=0).astype(BF16)
+    column_tenant = lax.broadcasted_iota(jnp.int32, (n, tenants * RANK), 1) // RANK
+    low = lax.dot_general(head_out, oa[...].reshape(tenants * RANK, oa.shape[2]), NT, preferred_element_type=F32)
+    low = jnp.where(tenant_of == column_tenant, low, 0.0)
+    low_out = jnp.concatenate(split3(low), axis=0).astype(BF16)
     adapter_up = ob[...].reshape(tenants * RANK, D)
     width = D // PARTS
     for c in range(PARTS // 2):
@@ -247,7 +276,7 @@
         o_copies[q - 1].wait_recv()
         result = result + out_recv[q].astype(F32)
     out_ref[...] = result.astype(BF16)
-    for copy in q_copies + p_copies + o_copies:
+    for copy in list(q_copies.values()) + p_copies + o_copies:
         copy.wait_send()
 
 
@@ -290,7 +319,7 @@
             pltpu.VMEM((D // PARTS // 128, PARTS * n, 128), F32),
             pltpu.VMEM((n, PARTS, D // PARTS), BF16),
             pltpu.VMEM((n, PARTS, D // PARTS), BF16),
-            dma((8,)), dma((n,)), dma((n,)), dma((n // GROUP, n)), dma((n // GROUP, n)), dma((n,)), dma((n,)),
+            dma((5,)), dma((6,)), dma((n,)), dma((n,)), dma((n // GROUP, n)), dma((n // GROUP, n)), dma((n,)), dma((n,)),
         ],
         compiler_params=pltpu.CompilerParams(
             collective_id=0, has_side_effects=True, vmem_limit_bytes=60 << 20),

time: 36.9 us -> 32.3 us (0.88)
  Pallas kernels: 35.3 us -> 30.7 us
    pallas_call x1, Pallas kernels: 35.3 us -> 30.7 us  [on_device(): pl.pallas_call(functools.partial(kernel, n), out_shape=jax.ShapeDtypeStru...]
where the time goes in v3:
time: 32.3 us; the launch traced here: 32.1 us
  Pallas kernels  30.7 us (95%)
  local copies, waits for them, and re-layouts  1.34 us (4%)
    pallas_call x1, Pallas kernels, on_device(): pl.pallas_call(functools.partial(kernel, n), out_shape=jax.ShapeDtypeStru...  30.7 us
    unnamed x1, local copies, waits for them, and re-layouts  1.34 us

profile of v3, /device:TPU:0, one launch (start us, length us, event | category | flops | bytes accessed | tf_op | source)
XLA Modules:
  0.0 32.1 jit_solution(15194739409871165887)
XLA Ops:
  0.0 30.7 %shard_map.136 = bf16[8,896]{1,0:T(8,128)(2,1)} custom-call(s32[8]{0:T(128)} %tenant_ref.1, s32[1,4]{1,0:T(1,128)} %length_ref.1, bf16[1,36864]{1,0:T(2,128)(2,1)} %base_ref.1, bf16[1,1536]{1,0:T(2,128)(2,1)} %latent_ref.1, bf16[4,16,1536]{2,1,0:T(8,128)(2,1)} %bitcast.9, bf16[4,16,36864]{2,1,0:T(8,128)(2,1)} %qb_hbm.1, bf16[576,4096]{1,0:T(8,128)(2,1)} %bitcast.7, ...), custom_call_target="tpu_custom_call" | custom-call | tf_op jit(solution)/shard_map/pallas_call | solution.py:298
  30.7 1.3 %copy.15 = bf16[1,1,8,896]{3,1,2,0:T(2,128)(2,1)} copy(bf16[1,1,8,896]{3,2,1,0:T(8,128)(2,1)} %bitcast.11) | data formatting | bytes 28672
